TPU v7x, 32 devices: a whole 2x2x4 slice. The times are simulated.
32 devices in a mesh: dp: 8 (over z, x), ctx: 4 (over y, core).
Axes of the slice: x: 2, y: 2, z: 4, core: 2. Of those that a mesh axis runs over, the one named last changes fastest.
Arguments:
- block_input: bfloat16 [8, 512, 1024], P('dp', 'ctx'), may hold values from -6 to 6
- segment_ids: int32 [8, 512], P('dp'), may hold values from 0 to 2, never falling along the last dimension, each value on 1 to 320 neighbouring positions
- ln1_gain: bfloat16 [1024], P('dp'), may hold values from 0.25 to 1.75
- ln1_bias: bfloat16 [1024], P('dp'), may hold values from -3 to 3
- qkv_weight: bfloat16 [1024, 3, 1024], P('dp', None, 'ctx'), may hold values from -3 to 3
- query_bias: bfloat16 [1024], P('dp'), may hold values from -3 to 3
- value_bias: bfloat16 [1024], P('dp'), may hold values from -1.1953125 to 1.1953125
- proj_weight: bfloat16 [1024, 1024], P('ctx', 'dp'), may hold values from -0.75 to 0.75
- proj_bias: bfloat16 [1024], P('dp'), may hold values from -3 to 3
- ln2_gain: bfloat16 [1024], P('dp'), may hold values from 0.25 to 1.75
- ln2_bias: bfloat16 [1024], P('dp'), may hold values from -3 to 3
- fc_weight: bfloat16 [1024, 4096], P('dp', 'ctx'), may hold values from -0.1875 to 0.1875
- fc_bias: bfloat16 [4096], P('dp'), may hold values from -3 to 3
- out_weight: bfloat16 [4096, 1024], P('ctx', 'dp'), may hold values from -0.09375 to 0.09375
- out_bias: bfloat16 [1024], P('dp'), may hold values from -3 to 3
- cotangent: bfloat16 [8, 512, 1024], P('dp', 'ctx'), may hold values from -6 to 6
Outputs:
- block_output: bfloat16 [8, 512, 1024], P('dp', 'ctx')
- input_grad: float32 [8, 512, 1024], P('dp', 'ctx')
- ln1_gain_grad: float32 [1024], P('dp')
- ln1_bias_grad: float32 [1024], P('dp')
- qkv_weight_grad: float32 [1024, 3, 1024], P('dp', None, 'ctx')
- query_bias_grad: float32 [1024], P('dp')
- value_bias_grad: float32 [1024], P('dp')
- proj_weight_grad: float32 [1024, 1024], P('ctx', 'dp')
- proj_bias_grad: float32 [1024], P('dp')
- ln2_gain_grad: float32 [1024], P('dp')
- ln2_bias_grad: float32 [1024], P('dp')
- fc_weight_grad: float32 [1024, 4096], P('dp', 'ctx')
- fc_bias_grad: float32 [4096], P('dp')
- out_weight_grad: float32 [4096, 1024], P('ctx', 'dp')
- out_bias_grad: float32 [1024], P('dp')
Inputs may be any that keep to these rules, and one draw needn't show every extreme that they name: `segment_ids`: segment numbers never fall along a sequence.
All inputs are finite; a program needn't handle non-finite values.
Results may differ from a plain program's by a relative error of at most 0.019.
Values may be sent and summed in bfloat16 or wider, within the bound.
A program may use at most 128 MiB of HBM per device.

v0:
```python
import jax
import jax.numpy as jnp
from jax import lax
from jax.sharding import PartitionSpec as P

D = 1024
HD = 64
FF = 4096
NORM_EPS = 1e-05
GELU_ROOT = 0.7978845608028654
GELU_CUBE = 0.044715
MASK_VALUE = -1e30


def norm_forward(residual):
    row_mean = jnp.mean(residual, axis=-1, keepdims=True)
    centered = residual - row_mean
    row_var = jnp.mean(centered * centered, axis=-1, keepdims=True)
    inv_std = lax.rsqrt(row_var + NORM_EPS)
    return (centered * inv_std, inv_std)


def norm_backward(grad_in, normed, inv_std, gain):
    scaled = grad_in * gain
    mean_scaled = jnp.mean(scaled, axis=-1, keepdims=True)
    mean_cross = jnp.mean(scaled * normed, axis=-1, keepdims=True)
    return inv_std * (scaled - mean_scaled - normed * mean_cross)


def gelu_pair(pre_act):
    inner_arg = GELU_ROOT * (pre_act + GELU_CUBE * pre_act * pre_act * pre_act)
    tangent = jnp.tanh(inner_arg)
    activated = 0.5 * pre_act * (1.0 + tangent)
    gelu_slope = 0.5 * (1.0 + tangent) + 0.5 * pre_act * (1.0 - tangent * tangent) * GELU_ROOT * (
        1.0 + 3.0 * GELU_CUBE * pre_act * pre_act
    )
    return (activated, gelu_slope)


def masked_scores(query_heads, key_heads, allowed):
    raw_scores = jnp.einsum(
        "qhd,khd->hqk", query_heads, key_heads, preferred_element_type=jnp.float32
    ) * HD ** (-0.5)
    return jnp.where(allowed[None], raw_scores, MASK_VALUE)


def attend(query_heads, key_heads, value_heads, allowed):
    scores = masked_scores(query_heads, key_heads, allowed)
    top_score = jnp.max(scores, axis=-1, keepdims=True)
    log_total = top_score + jnp.log(jnp.sum(jnp.exp(scores - top_score), axis=-1, keepdims=True))
    attn_probs = jnp.where(allowed[None], jnp.exp(scores - log_total), 0.0)
    probs_half = attn_probs.astype(jnp.bfloat16)
    attended = jnp.einsum(
        "hqk,khd->qhd", probs_half, value_heads, preferred_element_type=jnp.float32
    )
    return (attended.reshape(query_heads.shape[0], -1).astype(jnp.bfloat16), log_total)


def attend_back(query_heads, key_heads, value_heads, allowed, log_total, grad_heads):
    scores = masked_scores(query_heads, key_heads, allowed)
    attn_probs = jnp.where(allowed[None], jnp.exp(scores - log_total), 0.0)
    probs_half = attn_probs.astype(jnp.bfloat16)
    prob_grad = jnp.einsum(
        "qhd,khd->hqk", grad_heads, value_heads, preferred_element_type=jnp.float32
    )
    value_part = jnp.einsum(
        "hqk,qhd->khd", probs_half, grad_heads, preferred_element_type=jnp.float32
    )
    delta_rows = jnp.sum(attn_probs * prob_grad, axis=-1, keepdims=True)
    score_grad = (attn_probs * (prob_grad - delta_rows) * HD ** (-0.5)).astype(jnp.bfloat16)
    query_grad = jnp.einsum(
        "hqk,khd->qhd", score_grad, key_heads, preferred_element_type=jnp.float32
    )
    key_part = jnp.einsum(
        "hqk,qhd->khd", score_grad, query_heads, preferred_element_type=jnp.float32
    )
    key_count = key_heads.shape[0]
    return (
        query_grad.reshape(query_heads.shape[0], -1),
        key_part.reshape(key_count, -1),
        value_part.reshape(key_count, -1),
    )


def place_part(part, whole_len, start):
    return lax.dynamic_update_slice_in_dim(jnp.zeros((whole_len,), jnp.float32), part, start, 0)


def body(
    block_input,
    segment_ids,
    ln1_gain,
    ln1_bias,
    qkv_weight,
    query_bias,
    value_bias,
    proj_weight,
    proj_bias,
    ln2_gain,
    ln2_bias,
    fc_weight,
    fc_bias,
    out_weight,
    out_bias,
    cotangent,
):
    tokens = block_input[0]
    seg_whole = segment_ids[0]
    grad_rows = cotangent[0]
    seq_length = seg_whole.shape[0]
    ctx_rank = lax.axis_index("ctx")
    key_pos = jnp.arange(seq_length, dtype=jnp.int32)
    resid_in = tokens.astype(jnp.float32)
    normed_one, inv_one = norm_forward(resid_in)
    grad_out = grad_rows.astype(jnp.float32)
    out_shift_grad = jnp.sum(grad_out, axis=0)
    vectors = lax.all_gather(
        jnp.concatenate(
            [
                ln1_gain,
                ln1_bias,
                query_bias,
                value_bias,
                proj_bias,
                ln2_gain,
                ln2_bias,
                out_bias,
                fc_bias,
            ]
        ),
        "dp",
        axis=0,
    )
    slice_len = ln1_gain.shape[0]
    dp_size = vectors.shape[0]
    ff_whole = fc_bias.shape[0] * dp_size

    def vector(at):
        return vectors[:, at * slice_len : (at + 1) * slice_len].astype(jnp.float32).reshape(-1)

    qkv_cols = lax.all_gather(qkv_weight, "dp", axis=0, tiled=True).reshape(D, -1)
    proj_rows = lax.all_gather(proj_weight, "dp", axis=1, tiled=True)
    fc_cols = lax.all_gather(fc_weight, "dp", axis=0, tiled=True)
    out_rows = lax.all_gather(out_weight, "dp", axis=1, tiled=True)
    quarter = proj_rows.shape[0]
    unit_part = fc_cols.shape[1]
    gain_first = vector(0)
    shift_first = vector(1)
    query_shift = lax.dynamic_slice_in_dim(vector(2), ctx_rank * quarter, quarter)
    value_shift = lax.dynamic_slice_in_dim(vector(3), ctx_rank * quarter, quarter)
    proj_shift = vector(4)
    gain_second = vector(5)
    shift_second = vector(6)
    out_shift = vector(7)
    fc_shift = lax.dynamic_slice_in_dim(
        vectors[:, 8 * slice_len :].astype(jnp.float32).reshape(-1), ctx_rank * unit_part, unit_part
    )
    local_heads = quarter // HD
    allowed = (key_pos[:, None] >= key_pos[None, :]) & (seg_whole[:, None] == seg_whole[None, :])
    hidden_one = (normed_one * gain_first + shift_first).astype(jnp.bfloat16)
    hidden_all, grad_all = (
        lax.all_gather(hidden_one, "ctx", axis=0, tiled=True),
        lax.all_gather(grad_rows, "ctx", axis=0, tiled=True),
    )
    qkv_out = jnp.dot(hidden_all, qkv_cols, preferred_element_type=jnp.float32)
    queries = (qkv_out[:, :quarter] + query_shift).astype(jnp.bfloat16)
    keys_here = qkv_out[:, quarter : 2 * quarter].astype(jnp.bfloat16)
    values_here = (qkv_out[:, 2 * quarter :] + value_shift).astype(jnp.bfloat16)
    query_heads = queries.reshape(seq_length, local_heads, HD)
    key_heads = keys_here.reshape(seq_length, local_heads, HD)
    value_heads = values_here.reshape(seq_length, local_heads, HD)
    attended, log_total = attend(query_heads, key_heads, value_heads, allowed)
    resid_mid = (
        resid_in
        + lax.psum_scatter(
            jnp.dot(attended, proj_rows, preferred_element_type=jnp.float32).astype(jnp.bfloat16),
            "ctx",
            scatter_dimension=0,
            tiled=True,
        ).astype(jnp.float32)
        + proj_shift
    )
    normed_two, inv_two = norm_forward(resid_mid)
    hidden_two = (normed_two * gain_second + shift_second).astype(jnp.bfloat16)
    hidden_two_all = lax.all_gather(hidden_two, "ctx", axis=0, tiled=True)
    pre_act = jnp.dot(hidden_two_all, fc_cols, preferred_element_type=jnp.float32) + fc_shift
    activated, gelu_slope = gelu_pair(pre_act)
    activated = activated.astype(jnp.bfloat16)
    block_output = (
        resid_mid
        + lax.psum_scatter(
            jnp.dot(activated, out_rows, preferred_element_type=jnp.float32).astype(jnp.bfloat16),
            "ctx",
            scatter_dimension=0,
            tiled=True,
        ).astype(jnp.float32)
        + out_shift
    ).astype(jnp.bfloat16)
    out_weight_grad = jnp.dot(activated.T, grad_all, preferred_element_type=jnp.float32)
    pre_grad = jnp.dot(grad_all, out_rows.T, preferred_element_type=jnp.float32) * gelu_slope
    fc_shift_grad = place_part(jnp.sum(pre_grad, axis=0), ff_whole, ctx_rank * unit_part)
    pre_grad_half = pre_grad.astype(jnp.bfloat16)
    fc_weight_grad = jnp.dot(hidden_two_all.T, pre_grad_half, preferred_element_type=jnp.float32)
    hidden_two_grad = lax.psum_scatter(
        jnp.dot(pre_grad_half, fc_cols.T, preferred_element_type=jnp.float32).astype(jnp.bfloat16),
        "ctx",
        scatter_dimension=0,
        tiled=True,
    ).astype(jnp.float32)
    gain_second_grad = jnp.sum(hidden_two_grad * normed_two, axis=0)
    shift_second_grad = jnp.sum(hidden_two_grad, axis=0)
    mid_grad = grad_out + norm_backward(hidden_two_grad, normed_two, inv_two, gain_second)
    proj_shift_grad = jnp.sum(mid_grad, axis=0)
    mid_grad_half = mid_grad.astype(jnp.bfloat16)
    mid_all = lax.all_gather(mid_grad_half, "ctx", axis=0, tiled=True)
    proj_weight_grad = jnp.dot(attended.T, mid_all, preferred_element_type=jnp.float32)
    attended_grad = jnp.dot(mid_all, proj_rows.T, preferred_element_type=jnp.float32).astype(
        jnp.bfloat16
    )
    grad_heads = attended_grad.reshape(seq_length, local_heads, HD)
    query_grad, key_grad, value_grad = attend_back(
        query_heads, key_heads, value_heads, allowed, log_total, grad_heads
    )
    query_shift_grad = place_part(jnp.sum(query_grad, axis=0), D, ctx_rank * quarter)
    value_shift_grad = place_part(jnp.sum(value_grad, axis=0), D, ctx_rank * quarter)
    qkv_grad = jnp.concatenate([query_grad, key_grad, value_grad], axis=1).astype(jnp.bfloat16)
    qkv_weight_grad = jnp.dot(hidden_all.T, qkv_grad, preferred_element_type=jnp.float32).reshape(
        D, 3, quarter
    )
    hidden_one_grad = lax.psum_scatter(
        jnp.dot(qkv_grad, qkv_cols.T, preferred_element_type=jnp.float32).astype(jnp.bfloat16),
        "ctx",
        scatter_dimension=0,
        tiled=True,
    ).astype(jnp.float32)
    gain_first_grad = jnp.sum(hidden_one_grad * normed_one, axis=0)
    shift_first_grad = jnp.sum(hidden_one_grad, axis=0)
    input_grad = mid_grad + norm_backward(hidden_one_grad, normed_one, inv_one, gain_first)
    half = jnp.bfloat16
    matrix_sums = (
        lax.psum_scatter(qkv_weight_grad.astype(half), "dp", scatter_dimension=0, tiled=True),
        lax.psum_scatter(proj_weight_grad.astype(half), "dp", scatter_dimension=1, tiled=True),
        lax.psum_scatter(fc_weight_grad.astype(half), "dp", scatter_dimension=0, tiled=True),
        lax.psum_scatter(out_weight_grad.astype(half), "dp", scatter_dimension=1, tiled=True),
    )
    matrix_sums = tuple((m.astype(jnp.float32) for m in matrix_sums))
    packed = jnp.concatenate(
        [
            v.reshape(dp_size, -1)
            for v in (
                gain_first_grad,
                shift_first_grad,
                query_shift_grad,
                value_shift_grad,
                proj_shift_grad,
                gain_second_grad,
                shift_second_grad,
                out_shift_grad,
                fc_shift_grad,
            )
        ],
        axis=1,
    )
    packed = lax.psum(packed, ("dp", "ctx"))
    mine = lax.dynamic_index_in_dim(packed, lax.axis_index("dp"), 0, keepdims=False)
    order = (0, 1, 2, 3, 4, 5, 6, 8, 7)
    pieces = [mine[i * slice_len : (i + 1) * slice_len] for i in range(8)] + [mine[8 * slice_len :]]
    vector_sums = tuple((pieces[i] for i in order))
    return (
        block_output[None],
        input_grad[None],
        vector_sums[0],
        vector_sums[1],
        matrix_sums[0],
        vector_sums[2],
        vector_sums[3],
        matrix_sums[1],
        vector_sums[4],
        vector_sums[5],
        vector_sums[6],
        matrix_sums[2],
        vector_sums[7],
        matrix_sums[3],
        vector_sums[8],
    )


def solution(mesh):
    return jax.shard_map(
        body,
        mesh=mesh,
        in_specs=(
            P("dp", "ctx", None),
            P("dp", None),
            P("dp"),
            P("dp"),
            P("dp", None, "ctx"),
            P("dp"),
            P("dp"),
            P("ctx", "dp"),
            P("dp"),
            P("dp"),
            P("dp"),
            P("dp", "ctx"),
            P("dp"),
            P("ctx", "dp"),
            P("dp"),
            P("dp", "ctx", None),
        ),
        out_specs=(
            P("dp", "ctx", None),
            P("dp", "ctx", None),
            P("dp"),
            P("dp"),
            P("dp", None, "ctx"),
            P("dp"),
            P("dp"),
            P("ctx", "dp"),
            P("dp"),
            P("dp"),
            P("dp"),
            P("dp", "ctx"),
            P("dp"),
            P("ctx", "dp"),
            P("dp"),
        ),
        check_vma=False,
    )
```

profile of v0, /device:TPU:0, one launch (start us, length us, event | category | flops | bytes accessed | tf_op | source)
XLA Modules:
  0.0 677.9 jit_solution(5925180839455593192)
XLA Ops:
  16.9 32.6 %all-gather.2 = bf16[8,1,1536]{2,1,0:T(2,128)(2,1)S(1)} all-gather(bf16[1,1,1536]{2,1,0:T(2,128)(2,1)S(1)} %reshape.258), channel_id=2, replica_groups=mesh['dp'=8,'ctx'=4] {'dp'}, dimensions={0}, use_global_device_ids=true | all-gather | bytes 27648 | tf_op jit(solution)/shard_map/all_gather | solution.py:117
  53.4 27.0 %all_gather.34 = bf16[256,1024]{1,0:T(8,128)(2,1)S(1)} all-gather(bf16[256,128]{1,0:T(8,128)(2,1)S(1)} %copy-done.4), channel_id=1, replica_groups=mesh['dp'=8,'ctx'=4] {'dp'}, dimensions={1}, use_global_device_ids=true | all-gather | bytes 589824 | tf_op jit(solution)/shard_map/all_gather | solution.py:142
  80.7 35.4 %all-gather.13.cloned.1.call-done = bf16[1024,3,256]{0,2,1:T(8,128)(2,1)} async-done(((bf16[128,3,256]{0,2,1:T(8,128)(2,1)}), bf16[1024,3,256]{0,2,1:T(8,128)(2,1)}) %all-gather.13.cloned.1.call-update) | async-done | bytes 1572880 | tf_op jit(solution)/shard_map/all_gather | solution.py:141
  116.2 2.7 fusion.84
  125.8 22.5 %reduce-scatter.13.cloned.1.call-done = bf16[128,1024]{1,0:T(8,128)(2,1)} async-done(((bf16[512,1024]{1,0:T(8,128)(2,1)}), bf16[128,1024]{1,0:T(8,128)(2,1)}) %reduce-scatter.13.cloned.1.call-update) | async-done | bytes 262160 | tf_op jit(solution)/shard_map/reduce_scatter | solution.py:175
  154.1 45.4 %all-gather.17.cloned.1.call-done = bf16[1024,1024]{1,0:T(8,128)(2,1)} async-done(((bf16[128,1024]{1,0:T(8,128)(2,1)}), bf16[1024,1024]{1,0:T(8,128)(2,1)}) %all-gather.17.cloned.1.call-update) | async-done | bytes 2097168 | tf_op jit(solution)/shard_map/all_gather | solution.py:143
  199.4 17.2 %all-gather.15.cloned.1.call-done = bf16[512,1024]{1,0:T(8,128)(2,1)} async-done(((bf16[128,1024]{1,0:T(8,128)(2,1)}), bf16[512,1024]{1,0:T(8,128)(2,1)}) %all-gather.15.cloned.1.call-update) | async-done | bytes 1048592 | tf_op jit(solution)/shard_map/all_gather | solution.py:185
  216.7 4.5 fusion.85
  221.2 13.7 %all-gather.23.cloned.1.call-done = bf16[1,512,1024]{2,1,0:T(8,128)(2,1)} async-done(((bf16[1,128,1024]{2,1,0:T(8,128)(2,1)}), bf16[1,512,1024]{2,1,0:T(8,128)(2,1)}) %all-gather.23.cloned.1.call-update) | async-done | bytes 1048592 | tf_op jit(solution)/shard_map/all_gather | solution.py:163
  234.8 52.4 %all-gather.19.cloned.1.call-done = bf16[1024,1024]{1,0:T(8,128)(2,1)} async-done(((bf16[1024,128]{1,0:T(8,128)(2,1)}), bf16[1024,1024]{1,0:T(8,128)(2,1)}) %all-gather.19.cloned.1.call-update) | async-done | bytes 2097168 | tf_op jit(solution)/shard_map/all_gather | solution.py:144
  287.2 5.1 fusion.83
  292.3 2.3 convolution_convert_fusion.4
  294.8 4.8 convolution_convert_fusion.5
  299.6 18.2 %reduce-scatter.17.cloned.1.call-done = bf16[128,1024]{1,0:T(8,128)(2,1)} async-done(((bf16[512,1024]{1,0:T(8,128)(2,1)}), bf16[128,1024]{1,0:T(8,128)(2,1)}) %reduce-scatter.17.cloned.1.call-update) | async-done | bytes 262160 | tf_op jit(solution)/shard_map/reduce_scatter | solution.py:204
  319.1 26.0 %reduce-scatter.15.cloned.1.call-done = bf16[128,1024]{1,0:T(8,128)(2,1)} async-done(((bf16[512,1024]{1,0:T(8,128)(2,1)}), bf16[128,1024]{1,0:T(8,128)(2,1)}) %reduce-scatter.15.cloned.1.call-update) | async-done | bytes 262160 | tf_op jit(solution)/shard_map/reduce_scatter | solution.py:191
  345.2 2.0 fusion.77
  348.0 4.8 convolution_convert_fusion
  352.9 4.0 copy.66
  357.0 4.2 convolution_convert_fusion.1
  361.2 3.6 all-gather.21.cloned.1.call-done
  369.2 2.7 fusion.86
  372.2 7.7 %fusion.22 = bf16[4,64,512]{2,1,0:T(8,128)(2,1)S(1)} fusion(bf16[512,4,64]{0,2,1:T(8,128)(2,1)S(1)} %bitcast.205, f32[4,512,512]{1,2,0:T(8,128)} %fusion.86, f32[4,512,512]{1,2,0:T(8,128)} %copy-done.1, f32[4,512]{1,0:T(4,128)S(1)} %log_add_fusion, pred[512,512]{0,1:T(8,128)(4,1)S(1)} %fusion.29), kind=kOutput, calls=%fused_computation.31 | convolution fusion | flops 147982848 | bytes 9183232 | tf_op jit(solution)/shard_map/hqk,qhd->khd/dot_general | solution.py:74
  379.9 9.0 %fusion.80 = (f32[4,64]{1,0:T(4,128)S(1)}, bf16[512,4,64]{0,2,1:T(8,128)(2,1)S(1)}) fusion(bf16[512,4,64]{0,2,1:T(8,128)(2,1)S(1)} %bitcast.203, f32[4,512,512]{1,2,0:T(8,128)} %fusion.86, f32[4,512]{1,0:T(4,128)S(1)} %log_add_fusion, f32[4,512,512]{1,2,0:T(8,128)} %copy-done.1, pred[512,512]{0,1:T(8,128)(4,1)S(1)} %fusion.29), kind=kOutput, calls=%fused_computation.144 | convolution fusion | flops 148113664 | bytes 9184256 | tf_op jit(solution)/shard_map/hqk,khd->qhd/dot_general | solution.py:71
  389.0 3.9 fusion.79
  395.0 2.4 convolution_convert_fusion.2
  399.9 37.2 %reduce-scatter.27.cloned.1.call-done = bf16[128,1024]{1,0:T(8,128)(2,1)} async-done(((bf16[1024,1024]{1,0:T(8,128)(2,1)}), bf16[128,1024]{1,0:T(8,128)(2,1)}) %reduce-scatter.27.cloned.1.call-update) | async-done | bytes 262160
  439.1 68.9 %reduce-scatter.23.cloned.1.call-done = bf16[128,1024]{1,0:T(8,128)(2,1)} async-done(((bf16[1024,1024]{1,0:T(8,128)(2,1)}), bf16[128,1024]{1,0:T(8,128)(2,1)}) %reduce-scatter.23.cloned.1.call-update) | async-done | bytes 262160 | tf_op jit(solution)/shard_map/reduce_scatter | solution.py:243
  509.8 63.9 %reduce-scatter.25.cloned.1.call-done = bf16[128,256]{1,0:T(8,128)(2,1)} async-done(((bf16[1024,256]{1,0:T(8,128)(2,1)}), bf16[128,256]{1,0:T(8,128)(2,1)}) %reduce-scatter.25.cloned.1.call-update) | async-done | bytes 65552
  575.3 24.6 %reduce-scatter.19.cloned.1.call-done = bf16[128,1024]{1,0:T(8,128)(2,1)} async-done(((bf16[512,1024]{1,0:T(8,128)(2,1)}), bf16[128,1024]{1,0:T(8,128)(2,1)}) %reduce-scatter.19.cloned.1.call-update) | async-done | bytes 262160 | tf_op jit(solution)/shard_map/reduce_scatter | solution.py:230
  601.2 40.2 %psum.7 = f32[8,1536]{1,0:T(8,128)S(1)} all-reduce(f32[8,1536]{1,0:T(8,128)S(1)} %constant_dynamic-update-slice_fusion), channel_id=1, replica_groups=mesh['dp'=8,'ctx'=4] {'dp','ctx'}, use_global_device_ids=true, to_apply=%region_24.25 | all-reduce | flops 12288 | bytes 98304 | tf_op jit(solution)/shard_map/psum | solution.py:264
  642.7 2.0 fusion.47
  644.7 25.0 %reduce-scatter.21.cloned.1.call-done = bf16[128,3,256]{2,0,1:T(8,128)(2,1)} async-done(((bf16[1024,3,256]{2,0,1:T(8,128)(2,1)}), bf16[128,3,256]{2,0,1:T(8,128)(2,1)}) %reduce-scatter.21.cloned.1.call-update) | async-done | bytes 196624 | tf_op jit(solution)/shard_map/reduce_scatter | solution.py:241
  (131 shorter events, 47.5 us)
Async XLA Ops:
  7.2 46.3 %copy-start.4 = (bf16[256,128]{1,0:T(8,128)(2,1)S(1)}, bf16[256,128]{1,0:T(8,128)(2,1)}, u32[]{:S(2)}) copy-start(bf16[256,128]{1,0:T(8,128)(2,1)} %param.23) | copy-start | bytes 196612
  7.2 73.3 %copy-start.5 = (s32[1,512]{1,0:T(1,128)S(1)}, s32[1,512]{1,0:T(1,128)}, u32[]{:S(2)}) copy-start(s32[1,512]{1,0:T(1,128)} %param.17) | copy-start | bytes 6148
  7.2 73.5 %all-gather.11.cloned.1.call-start = ((), (), s32[]{:S(2)}) async-start(), calls=%async_computation.8 | async-start | bytes 1310720 | tf_op jit(solution)/shard_map/all_gather | solution.py:162
  51.4 64.8 %all-gather.13.cloned.1.call-start = ((), (), s32[]{:S(2)}) async-start(), calls=%async_computation.9 | async-start | bytes 1769472 | tf_op jit(solution)/shard_map/all_gather | solution.py:141
  53.2 95.1 %reduce-scatter.13.cloned.1.call-start = ((), (), s32[]{:S(2)}) async-start(), calls=%async_computation.10 | async-start | bytes 1310720 | tf_op jit(solution)/shard_map/reduce_scatter | solution.py:175
  120.4 2.0 copy-start.1
  123.7 24.6 %copy-start = (bf16[1,128,1024]{2,1,0:T(8,128)(2,1)S(1)}, bf16[1,128,1024]{2,1,0:T(8,128)(2,1)}, u32[]{:S(2)}) copy-start(bf16[1,128,1024]{2,1,0:T(8,128)(2,1)} %param.16) | copy-start | bytes 786436
  125.2 74.2 %all-gather.17.cloned.1.call-start = ((), (), s32[]{:S(2)}) async-start(), calls=%async_computation.12 | async-start | bytes 2359296 | tf_op jit(solution)/shard_map/all_gather | solution.py:143
  125.8 90.9 %all-gather.15.cloned.1.call-start = ((), (), s32[]{:S(2)}) async-start(), calls=%async_computation.11 | async-start | bytes 1310720 | tf_op jit(solution)/shard_map/all_gather | solution.py:185
  152.5 82.4 %all-gather.23.cloned.1.call-start = ((), (), s32[]{:S(2)}) async-start(), calls=%async_computation.20 | async-start | bytes 1310720 | tf_op jit(solution)/shard_map/all_gather | solution.py:163
  153.0 134.2 %all-gather.19.cloned.1.call-start = ((), (), s32[]{:S(2)}) async-start(), calls=%async_computation.13 | async-start | bytes 2359296 | tf_op jit(solution)/shard_map/all_gather | solution.py:144
  153.8 164.0 %reduce-scatter.17.cloned.1.call-start = ((), (), s32[]{:S(2)}) async-start(), calls=%async_computation.15 | async-start | bytes 1310720 | tf_op jit(solution)/shard_map/reduce_scatter | solution.py:204
  287.2 5.1 copy-start.6
  292.3 2.4 copy-start.10
  294.7 23.1 %copy-start.2 = (bf16[128,1024]{1,0:T(8,128)(2,1)S(1)}, bf16[128,1024]{1,0:T(8,128)(2,1)}, u32[]{:S(2)}) copy-start(bf16[128,1024]{1,0:T(8,128)(2,1)} %reduce-scatter.13.cloned.1.call-done) | copy-start | bytes 786436
  294.7 50.5 %copy-start.3 = (bf16[1,128,1024]{2,1,0:T(8,128)(2,1)S(1)}, bf16[1,128,1024]{2,1,0:T(8,128)(2,1)}, u32[]{:S(2)}) copy-start(bf16[1,128,1024]{2,1,0:T(8,128)(2,1)} %param.31) | copy-start | bytes 786436
  294.7 50.5 %reduce-scatter.15.cloned.1.call-start = ((), (), s32[]{:S(2)}) async-start(), calls=%async_computation.14 | async-start | bytes 1310720 | tf_op jit(solution)/shard_map/reduce_scatter | solution.py:191
  299.6 65.3 %all-gather.21.cloned.1.call-start = ((), (), s32[]{:S(2)}) async-start(), calls=%async_computation.16 | async-start | bytes 1310720 | tf_op jit(solution)/shard_map/all_gather | solution.py:215
  348.0 89.1 %reduce-scatter.27.cloned.1.call-start = ((), (), s32[]{:S(2)}) async-start(), calls=%async_computation.22 | async-start | bytes 2359296
  356.9 151.1 %reduce-scatter.23.cloned.1.call-start = ((), (), s32[]{:S(2)}) async-start(), calls=%async_computation.19 | async-start | bytes 2359296 | tf_op jit(solution)/shard_map/reduce_scatter | solution.py:243
  361.2 212.5 %reduce-scatter.25.cloned.1.call-start = ((), (), s32[]{:S(2)}) async-start(), calls=%async_computation.21 | async-start | bytes 589824
  371.9 227.9 %reduce-scatter.19.cloned.1.call-start = ((), (), s32[]{:S(2)}) async-start(), calls=%async_computation.17 | async-start | bytes 1310720 | tf_op jit(solution)/shard_map/reduce_scatter | solution.py:230
  388.9 3.9 copy-start.8
  389.0 3.9 copy-start.7
  392.9 2.0 copy-start.9
  394.9 274.7 %reduce-scatter.21.cloned.1.call-start = ((), (), s32[]{:S(2)}) async-start(), calls=%async_computation.18 | async-start | bytes 1769472 | tf_op jit(solution)/shard_map/reduce_scatter | solution.py:241
Sparse Core Ops, SparseCore 0:
  51.5 17.5 all-gather.10
  71.7 44.3 all-gather.12
  125.3 22.9 reduce-scatter.12
  150.3 49.0 all-gather.16
  201.4 15.2 all-gather.14
  218.1 16.6 all-gather.22
  236.9 50.3 all-gather.18
  294.8 22.9 reduce-scatter.16
  320.4 24.7 reduce-scatter.14
  348.1 16.6 all-gather.20
  368.4 68.6 reduce-scatter.26
  440.5 67.4 reduce-scatter.22
  511.9 61.6 reduce-scatter.24
  576.0 23.7 reduce-scatter.18
  603.1 66.4 reduce-scatter.20
where the time goes:
time: 679 us; the launch traced here: 678 us
  waiting for transfers between devices  456 us (67%)
  blocking collectives  99.8 us (15%)
  matrix products  63.1 us (9%)
  other arithmetic  21.9 us (3%)
  local copies, waits for them, and re-layouts  21.7 us (3%)
  between operations  14.3 us (2%)
    unnamed x17, waiting for transfers between devices  103 us
    reduce_scatter x1, waiting for transfers between devices, body(): lax.psum_scatter(fc_weight_grad.astype(half), 'dp', scatter_dimension=0,...  68.9 us
    all_gather x1, waiting for transfers between devices, body(): out_rows = lax.all_gather(out_weight, 'dp', axis=1, tiled=True)  52.4 us
    all_gather x1, waiting for transfers between devices, body(): fc_cols = lax.all_gather(fc_weight, 'dp', axis=0, tiled=True)  45.4 us
    psum x1, blocking collectives, body(): packed = lax.psum(packed, ('dp', 'ctx'))  40.2 us
    all_gather x1, waiting for transfers between devices, body(): lax.all_gather(qkv_weight, 'dp', axis=0, tiled=True).reshape(D, -1)  35.4 us
    all_gather x1, blocking collectives, body(): lax.all_gather(jnp.concatenate([ln1_gain, ln1_bias, query_bias, value_bia...  32.6 us
    all_gather x1, blocking collectives, body(): proj_rows = lax.all_gather(proj_weight, 'dp', axis=1, tiled=True)  27 us
  transfers between devices with their start and end apart: 15, of which 14 were waited for; matrix products, arithmetic and copies ran while one was open for 11% of the time, Pallas kernels for 0%

commit v1 on v0

--- a/solution.py
+++ b/solution.py
@@ -261,7 +261,7 @@
         ],
         axis=1,
     )
-    packed = lax.psum(packed, ("dp", "ctx"))
+    packed = jnp.sum(lax.all_gather(packed, ("dp", "ctx")), axis=0)
     mine = lax.dynamic_index_in_dim(packed, lax.axis_index("dp"), 0, keepdims=False)
     order = (0, 1, 2, 3, 4, 5, 6, 8, 7)
     pieces = [mine[i * slice_len : (i + 1) * slice_len] for i in range(8)] + [mine[8 * slice_len :]]

time: 679 us -> 763 us (1.12)
  waiting for transfers between devices: 456 us -> 576 us
  blocking collectives: 99.8 us -> 59.6 us
    all_gather x0 -> x1, waiting for transfers between devices: none -> 54.9 us  [body(): packed = jnp.sum(lax.all_gather(packed, ('dp', 'ctx')), axis=0)]
    reduce_scatter x1, waiting for transfers between devices: 25 us -> 65.7 us  [body(): lax.psum_scatter(qkv_weight_grad.astype(half), 'dp', scatter_dimension=0,...]
    psum x1 -> x0, blocking collectives: 40.2 us -> none  [body(): packed = lax.psum(packed, ('dp', 'ctx'))]
    unnamed x17 -> x18, waiting for transfers between devices: 103 us -> 136 us
    reduce_scatter x1, waiting for transfers between devices: 24.6 us -> 2.95 us  [body(): lax.psum_scatter(jnp.dot(qkv_grad, qkv_cols.T, preferred_element_type=jnp...]
    all_gather x1, waiting for transfers between devices: 3.64 us -> 16.6 us  [body(): mid_all = lax.all_gather(mid_grad_half, 'ctx', axis=0, tiled=True)]
    unnamed x46 -> x54, local copies, waits for them, and re-layouts: 16.7 us -> 20.5 us
  transfers between devices with their start and end apart: 15 -> 16, of which waited for: 14 -> 15; matrix products, arithmetic and copies ran while one was open for 11% -> 6% of each run, Pallas kernels for 0% -> 0%
where the time goes in v1:
time: 763 us; the launch traced here: 762 us
  waiting for transfers between devices  576 us (75%)
  matrix products  62.7 us (8%)
  blocking collectives  59.6 us (8%)
  local copies, waits for them, and re-layouts  25.5 us (3%)
  other arithmetic  22.5 us (3%)
  between operations  14.3 us (2%)
    unnamed x18, waiting for transfers between devices  136 us
    reduce_scatter x1, waiting for transfers between devices, body(): lax.psum_scatter(fc_weight_grad.astype(half), 'dp', scatter_dimension=0,...  69 us
    reduce_scatter x1, waiting for transfers between devices, body(): lax.psum_scatter(qkv_weight_grad.astype(half), 'dp', scatter_dimension=0,...  65.7 us
    all_gather x1, waiting for transfers between devices, body(): packed = jnp.sum(lax.all_gather(packed, ('dp', 'ctx')), axis=0)  54.9 us
    all_gather x1, waiting for transfers between devices, body(): out_rows = lax.all_gather(out_weight, 'dp', axis=1, tiled=True)  52.4 us
    all_gather x1, waiting for transfers between devices, body(): fc_cols = lax.all_gather(fc_weight, 'dp', axis=0, tiled=True)  45.4 us
    all_gather x1, waiting for transfers between devices, body(): lax.all_gather(qkv_weight, 'dp', axis=0, tiled=True).reshape(D, -1)  35.4 us
    all_gather x1, blocking collectives, body(): lax.all_gather(jnp.concatenate([ln1_gain, ln1_bias, query_bias, value_bia...  32.6 us
  transfers between devices with their start and end apart: 16, of which 15 were waited for; matrix products, arithmetic and copies ran while one was open for 6% of the time, Pallas kernels for 0%

profile of v1, /device:TPU:0, one launch (start us, length us, event | category | flops | bytes accessed | tf_op | source)
XLA Modules:
  0.0 761.7 jit_solution(7486782388946372886)
XLA Ops:
  16.9 32.6 %all-gather.3 = bf16[8,1,1536]{2,1,0:T(2,128)(2,1)S(1)} all-gather(bf16[1,1,1536]{2,1,0:T(2,128)(2,1)S(1)} %reshape.259), channel_id=2, replica_groups=mesh['dp'=8,'ctx'=4] {'dp'}, dimensions={0}, use_global_device_ids=true | all-gather | bytes 27648 | tf_op jit(solution)/shard_map/all_gather | solution.py:117
  53.4 27.0 %all_gather.40 = bf16[256,1024]{1,0:T(8,128)(2,1)S(1)} all-gather(bf16[256,128]{1,0:T(8,128)(2,1)S(1)} %copy-done.6), channel_id=1, replica_groups=mesh['dp'=8,'ctx'=4] {'dp'}, dimensions={1}, use_global_device_ids=true | all-gather | bytes 589824 | tf_op jit(solution)/shard_map/all_gather | solution.py:142
  80.7 35.4 %all-gather.15.cloned.1.call-done = bf16[1024,3,256]{0,2,1:T(8,128)(2,1)} async-done(((bf16[128,3,256]{0,2,1:T(8,128)(2,1)}), bf16[1024,3,256]{0,2,1:T(8,128)(2,1)}) %all-gather.15.cloned.1.call-update) | async-done | bytes 1572880 | tf_op jit(solution)/shard_map/all_gather | solution.py:141
  116.2 2.7 fusion.84
  125.8 22.5 %reduce-scatter.13.cloned.1.call-done = bf16[128,1024]{1,0:T(8,128)(2,1)} async-done(((bf16[512,1024]{1,0:T(8,128)(2,1)}), bf16[128,1024]{1,0:T(8,128)(2,1)}) %reduce-scatter.13.cloned.1.call-update) | async-done | bytes 262160 | tf_op jit(solution)/shard_map/reduce_scatter | solution.py:175
  154.0 45.4 %all-gather.19.cloned.1.call-done = bf16[1024,1024]{1,0:T(8,128)(2,1)} async-done(((bf16[128,1024]{1,0:T(8,128)(2,1)}), bf16[1024,1024]{1,0:T(8,128)(2,1)}) %all-gather.19.cloned.1.call-update) | async-done | bytes 2097168 | tf_op jit(solution)/shard_map/all_gather | solution.py:143
  199.4 17.2 %all-gather.17.cloned.1.call-done = bf16[512,1024]{1,0:T(8,128)(2,1)} async-done(((bf16[128,1024]{1,0:T(8,128)(2,1)}), bf16[512,1024]{1,0:T(8,128)(2,1)}) %all-gather.17.cloned.1.call-update) | async-done | bytes 1048592 | tf_op jit(solution)/shard_map/all_gather | solution.py:185
  216.6 4.6 fusion.85
  221.2 13.6 %all-gather.25.cloned.1.call-done = bf16[1,512,1024]{2,1,0:T(8,128)(2,1)} async-done(((bf16[1,128,1024]{2,1,0:T(8,128)(2,1)}), bf16[1,512,1024]{2,1,0:T(8,128)(2,1)}) %all-gather.25.cloned.1.call-update) | async-done | bytes 1048592 | tf_op jit(solution)/shard_map/all_gather | solution.py:163
  234.8 52.4 %all-gather.21.cloned.1.call-done = bf16[1024,1024]{1,0:T(8,128)(2,1)} async-done(((bf16[1024,128]{1,0:T(8,128)(2,1)}), bf16[1024,1024]{1,0:T(8,128)(2,1)}) %all-gather.21.cloned.1.call-update) | async-done | bytes 2097168 | tf_op jit(solution)/shard_map/all_gather | solution.py:144
  287.2 5.1 fusion.83
  293.2 2.3 convolution_convert_fusion.4
  295.6 4.8 convolution_convert_fusion.5
  300.5 18.2 %reduce-scatter.17.cloned.1.call-done = bf16[128,1024]{1,0:T(8,128)(2,1)} async-done(((bf16[512,1024]{1,0:T(8,128)(2,1)}), bf16[128,1024]{1,0:T(8,128)(2,1)}) %reduce-scatter.17.cloned.1.call-update) | async-done | bytes 262160 | tf_op jit(solution)/shard_map/reduce_scatter | solution.py:204
  320.0 26.1 %reduce-scatter.15.cloned.1.call-done = bf16[128,1024]{1,0:T(8,128)(2,1)} async-done(((bf16[512,1024]{1,0:T(8,128)(2,1)}), bf16[128,1024]{1,0:T(8,128)(2,1)}) %reduce-scatter.15.cloned.1.call-update) | async-done | bytes 262160 | tf_op jit(solution)/shard_map/reduce_scatter | solution.py:191
  346.1 2.0 fusion.77
  349.1 16.6 %all-gather.23.cloned.1.call-done = bf16[512,1024]{1,0:T(8,128)(2,1)} async-done(((bf16[128,1024]{1,0:T(8,128)(2,1)}), bf16[512,1024]{1,0:T(8,128)(2,1)}) %all-gather.23.cloned.1.call-update) | async-done | bytes 1048592 | tf_op jit(solution)/shard_map/all_gather | solution.py:215
  367.4 3.7 fusion.79
  371.1 2.7 fusion.86
  373.8 7.5 fusion.22
  381.3 9.0 %fusion.80 = (f32[4,64]{1,0:T(4,128)S(1)}, bf16[512,4,64]{0,2,1:T(8,128)(2,1)S(1)}) fusion(bf16[512,4,64]{0,2,1:T(8,128)(2,1)S(1)} %bitcast.205, f32[4,512,512]{1,2,0:T(8,128)} %fusion.86, f32[4,512]{1,0:T(4,128)S(1)} %log_add_fusion, f32[4,512,512]{1,2,0:T(8,128)} %copy-done.1, pred[512,512]{0,1:T(8,128)(4,1)S(1)} %fusion.29), kind=kOutput, calls=%fused_computation.145 | convolution fusion | flops 148113664 | bytes 9184256 | tf_op jit(solution)/shard_map/hqk,khd->qhd/dot_general | solution.py:71
  390.4 3.5 convolution_convert_fusion.3
  394.0 4.8 convolution_convert_fusion
  398.8 4.1 copy.75
  404.0 3.8 convolution_convert_fusion.1
  410.9 2.5 convolution_convert_fusion.2
  415.9 2.9 reduce-scatter.19.cloned.1.call-done
  420.9 70.0 %reduce-scatter.27.cloned.1.call-done = bf16[128,1024]{1,0:T(8,128)(2,1)} async-done(((bf16[1024,1024]{1,0:T(8,128)(2,1)}), bf16[128,1024]{1,0:T(8,128)(2,1)}) %reduce-scatter.27.cloned.1.call-update) | async-done | bytes 262160
  492.9 69.0 %reduce-scatter.23.cloned.1.call-done = bf16[128,1024]{1,0:T(8,128)(2,1)} async-done(((bf16[1024,1024]{1,0:T(8,128)(2,1)}), bf16[128,1024]{1,0:T(8,128)(2,1)}) %reduce-scatter.23.cloned.1.call-update) | async-done | bytes 262160 | tf_op jit(solution)/shard_map/reduce_scatter | solution.py:243
  563.6 63.8 %reduce-scatter.25.cloned.1.call-done = bf16[128,256]{1,0:T(8,128)(2,1)} async-done(((bf16[1024,256]{1,0:T(8,128)(2,1)}), bf16[128,256]{1,0:T(8,128)(2,1)}) %reduce-scatter.25.cloned.1.call-update) | async-done | bytes 65552
  630.1 65.7 %reduce-scatter.21.cloned.1.call-done = bf16[128,3,256]{2,0,1:T(8,128)(2,1)} async-done(((bf16[1024,3,256]{2,0,1:T(8,128)(2,1)}), bf16[128,3,256]{2,0,1:T(8,128)(2,1)}) %reduce-scatter.21.cloned.1.call-update) | async-done | bytes 196624 | tf_op jit(solution)/shard_map/reduce_scatter | solution.py:241
  697.5 54.9 %all-gather.27.cloned.1.call-done = f32[256,1536]{1,0:T(8,128)} async-done(((f32[8,1536]{1,0:T(8,128)}), f32[256,1536]{1,0:T(8,128)}) %all-gather.27.cloned.1.call-update) | async-done | bytes 1572880 | tf_op jit(solution)/shard_map/all_gather | solution.py:264
  (142 shorter events, 51.1 us)
Async XLA Ops:
  7.2 46.3 %copy-start.6 = (bf16[256,128]{1,0:T(8,128)(2,1)S(1)}, bf16[256,128]{1,0:T(8,128)(2,1)}, u32[]{:S(2)}) copy-start(bf16[256,128]{1,0:T(8,128)(2,1)} %param.23) | copy-start | bytes 196612
  7.2 73.3 %copy-start.8 = (s32[1,512]{1,0:T(1,128)S(1)}, s32[1,512]{1,0:T(1,128)}, u32[]{:S(2)}) copy-start(s32[1,512]{1,0:T(1,128)} %param.17) | copy-start | bytes 6148
  7.2 73.5 %all-gather.13.cloned.1.call-start = ((), (), s32[]{:S(2)}) async-start(), calls=%async_computation.8 | async-start | bytes 1310720 | tf_op jit(solution)/shard_map/all_gather | solution.py:162
  51.4 64.8 %all-gather.15.cloned.1.call-start = ((), (), s32[]{:S(2)}) async-start(), calls=%async_computation.9 | async-start | bytes 1769472 | tf_op jit(solution)/shard_map/all_gather | solution.py:141
  53.2 95.1 %reduce-scatter.13.cloned.1.call-start = ((), (), s32[]{:S(2)}) async-start(), calls=%async_computation.10 | async-start | bytes 1310720 | tf_op jit(solution)/shard_map/reduce_scatter | solution.py:175
  120.4 1.9 copy-start.1
  123.7 24.6 %copy-start = (bf16[1,128,1024]{2,1,0:T(8,128)(2,1)S(1)}, bf16[1,128,1024]{2,1,0:T(8,128)(2,1)}, u32[]{:S(2)}) copy-start(bf16[1,128,1024]{2,1,0:T(8,128)(2,1)} %param.16) | copy-start | bytes 786436
  125.2 74.2 %all-gather.19.cloned.1.call-start = ((), (), s32[]{:S(2)}) async-start(), calls=%async_computation.12 | async-start | bytes 2359296 | tf_op jit(solution)/shard_map/all_gather | solution.py:143
  125.7 90.9 %all-gather.17.cloned.1.call-start = ((), (), s32[]{:S(2)}) async-start(), calls=%async_computation.11 | async-start | bytes 1310720 | tf_op jit(solution)/shard_map/all_gather | solution.py:185
  152.4 82.4 %all-gather.25.cloned.1.call-start = ((), (), s32[]{:S(2)}) async-start(), calls=%async_computation.20 | async-start | bytes 1310720 | tf_op jit(solution)/shard_map/all_gather | solution.py:163
  153.0 134.2 %all-gather.21.cloned.1.call-start = ((), (), s32[]{:S(2)}) async-start(), calls=%async_computation.13 | async-start | bytes 2359296 | tf_op jit(solution)/shard_map/all_gather | solution.py:144
  153.8 164.9 %reduce-scatter.17.cloned.1.call-start = ((), (), s32[]{:S(2)}) async-start(), calls=%async_computation.15 | async-start | bytes 1310720 | tf_op jit(solution)/shard_map/reduce_scatter | solution.py:204
  287.2 6.0 copy-start.9
  292.3 1.0 copy-start.14
  295.5 23.2 %copy-start.2 = (bf16[128,1024]{1,0:T(8,128)(2,1)S(1)}, bf16[128,1024]{1,0:T(8,128)(2,1)}, u32[]{:S(2)}) copy-start(bf16[128,1024]{1,0:T(8,128)(2,1)} %reduce-scatter.13.cloned.1.call-done) | copy-start | bytes 786436
  295.6 50.5 %copy-start.3 = (bf16[1,128,1024]{2,1,0:T(8,128)(2,1)S(1)}, bf16[1,128,1024]{2,1,0:T(8,128)(2,1)}, u32[]{:S(2)}) copy-start(bf16[1,128,1024]{2,1,0:T(8,128)(2,1)} %param.31) | copy-start | bytes 786436
  295.6 50.5 %reduce-scatter.15.cloned.1.call-start = ((), (), s32[]{:S(2)}) async-start(), calls=%async_computation.14 | async-start | bytes 1310720 | tf_op jit(solution)/shard_map/reduce_scatter | solution.py:191
  300.4 65.3 %all-gather.23.cloned.1.call-start = ((), (), s32[]{:S(2)}) async-start(), calls=%async_computation.16 | async-start | bytes 1310720 | tf_op jit(solution)/shard_map/all_gather | solution.py:215
  348.9 70.0 %reduce-scatter.19.cloned.1.call-start = ((), (), s32[]{:S(2)}) async-start(), calls=%async_computation.17 | async-start | bytes 1310720 | tf_op jit(solution)/shard_map/reduce_scatter | solution.py:230
  371.1 19.3 %copy-start.11 = (bf16[512,4,64]{0,2,1:T(8,128)(2,1)}, bf16[512,4,64]{0,2,1:T(8,128)(2,1)S(1)}, u32[]{:S(2)}) copy-start(bf16[512,4,64]{0,2,1:T(8,128)(2,1)S(1)} %get-tuple-element.29) | copy-start | bytes 786436
  381.3 9.1 %copy-start.12 = (bf16[4,64,512]{2,1,0:T(8,128)(2,1)}, bf16[4,64,512]{2,1,0:T(8,128)(2,1)S(1)}, u32[]{:S(2)}) copy-start(bf16[4,64,512]{2,1,0:T(8,128)(2,1)S(1)} %fusion.22) | copy-start | bytes 786436
  390.4 3.5 copy-start.13
  393.9 97.0 %reduce-scatter.27.cloned.1.call-start = ((), (), s32[]{:S(2)}) async-start(), calls=%async_computation.23 | async-start | bytes 2359296
  402.8 1.2 copy-start.10
  402.8 159.0 %reduce-scatter.23.cloned.1.call-start = ((), (), s32[]{:S(2)}) async-start(), calls=%async_computation.19 | async-start | bytes 2359296 | tf_op jit(solution)/shard_map/reduce_scatter | solution.py:243
  407.8 1.2 copy-start.4
  407.9 219.5 %reduce-scatter.25.cloned.1.call-start = ((), (), s32[]{:S(2)}) async-start(), calls=%async_computation.22 | async-start | bytes 589824
  410.5 285.3 %reduce-scatter.21.cloned.1.call-start = ((), (), s32[]{:S(2)}) async-start(), calls=%async_computation.18 | async-start | bytes 1769472 | tf_op jit(solution)/shard_map/reduce_scatter | solution.py:241
  414.9 337.4 %all-gather.27.cloned.1.call-start = ((), (), s32[]{:S(2)}) async-start(), calls=%async_computation.21 | async-start | bytes 1622016 | tf_op jit(solution)/shard_map/all_gather | solution.py:264
  418.9 210.1 %copy-start.5 = (bf16[128,1024]{1,0:T(8,128)(2,1)S(1)}, bf16[128,1024]{1,0:T(8,128)(2,1)}, u32[]{:S(2)}) copy-start(bf16[128,1024]{1,0:T(8,128)(2,1)} %reduce-scatter.19.cloned.1.call-done) | copy-start | bytes 786436
  420.3 0.6 copy-start.7
Sparse Core Ops, SparseCore 0:
  51.5 17.5 all-gather.12
  71.7 44.3 all-gather.14
  125.3 22.9 reduce-scatter.12
  150.3 49.0 all-gather.18
  201.4 15.2 all-gather.16
  218.0 16.6 all-gather.24
  236.8 50.3 all-gather.20
  295.7 22.9 reduce-scatter.16
  321.2 24.7 reduce-scatter.14
  349.0 16.6 all-gather.22
  394.0 24.7 reduce-scatter.18
  422.3 68.6 reduce-scatter.26
  494.4 67.3 reduce-scatter.22
  565.6 61.7 reduce-scatter.24
  630.7 65.0 reduce-scatter.20
  698.6 53.7 all-gather.26
